TPU v7x, 256 devices: a whole 4x4x8 slice. The times are simulated.
256 devices in a mesh: section: 8 (over z), ctx: 16 (over y, x_hi, core), tp: 2 (over x_lo).
Axes of the slice: x: 4 (x_hi: 2, x_lo: 2; x = x_hi * 2 + x_lo), y: 4, z: 8, core: 2. Of those that a mesh axis runs over, the one named last changes fastest.
Arguments:
- x_in: bfloat16 [2, 4096, 2688], P(None, ('ctx', 'tp')), may hold values from -180 to 180
- norm_gain: bfloat16 [8, 2688], P('section'), may hold values from 0.099609375 to 1.8984375
- w_query: bfloat16 [8, 2688, 2048], P('section', None, 'tp'), may hold values from -1 to 1
- w_key: bfloat16 [8, 2688, 1024], P('section', 'ctx', 'tp'), may hold values from -3 to 3
- value_projection: bfloat16 [8, 2688, 1024], P('section', 'ctx', 'tp'), may hold values from -0.125 to 0.125
- w_out: bfloat16 [8, 2048, 2688], P('section', 'tp', 'ctx'), may hold values from -0.125 to 0.125
- doc_ids: int32 [2, 32], replicated, may hold values from 0 to 7, never falling along the last dimension, each value on 1 to 6 neighbouring positions
Outputs:
- layer_out: bfloat16 [8, 2, 4096, 2688], P('section', None, ('ctx', 'tp'))
Inputs may be any that keep to these rules, and one draw needn't show every extreme that they name: Along each row doc_ids never falls, so each document covers whole consecutive blocks of 128 tokens.
All inputs are finite; a program needn't handle non-finite values.
Results may differ from a plain program's by a relative error of at most 0.018.
Values may be sent and summed in bfloat16 or wider, within the bound.
A program may use at most 128 MiB of HBM per device.

v0:
```python
import jax
import jax.numpy as jnp
from jax import lax
from jax.sharding import PartitionSpec as P

HEAD_SIZE = 128
WINDOW = 1024
BLOCK = 128


query_scale = 168.0 ** (-0.5)
rope_base = 10000.0


def shifted(shard, axis, by):
    count = lax.axis_size(axis)
    pairs = [(i, i + by) for i in range(count) if 0 <= i + by < count]
    return lax.ppermute(shard, axis, pairs)


def rms_normed(hidden, gain_row):
    widened = hidden.astype(jnp.float32)
    mean_square = jnp.mean(widened * widened, axis=-1, keepdims=True)
    return (widened * lax.rsqrt(mean_square + 1e-06) * gain_row.astype(jnp.float32)).astype(
        jnp.bfloat16
    )


def rotary_apply(tensor, token_position):
    half_dim = tensor.shape[-1] // 2
    frequency = rope_base ** (-(jnp.arange(half_dim, dtype=jnp.float32) * 2.0) / tensor.shape[-1])
    angles = token_position.astype(jnp.float32)[:, None] * frequency[None, :]
    cosine_table = jnp.cos(angles)[:, None, :]
    sine_table = jnp.sin(angles)[:, None, :]
    first_half = tensor[..., :half_dim]
    second_half = tensor[..., half_dim:]
    return jnp.concatenate(
        [
            first_half * cosine_table - second_half * sine_table,
            second_half * cosine_table + first_half * sine_table,
        ],
        axis=-1,
    )


def doc_lookup(ids_row, token_index, block):
    block_count = ids_row.shape[0]
    start_block = jnp.sum((ids_row[None, :] < ids_row[:, None]).astype(jnp.int32), axis=1)
    block_of = jnp.clip(token_index // block, 0, block_count - 1)
    onehot = (block_of[:, None] == jnp.arange(block_count, dtype=jnp.int32)[None, :]).astype(
        jnp.int32
    )
    start_of = jnp.sum(onehot * start_block[None, :], axis=1)
    doc_of = jnp.sum(onehot * ids_row[None, :], axis=1)
    return (token_index - start_of * block, doc_of)


def attention_rows(
    grouped_heads, key_matrix_rows, value_rows, query_index, query_doc, key_index, key_doc
):
    scores = (
        jnp.einsum(
            "qgrd,kgd->grqk", grouped_heads, key_matrix_rows, preferred_element_type=jnp.float32
        )
        * query_scale
    )
    allowed = (key_index[None, :] >= 0) & (key_index[None, :] <= query_index[:, None])
    allowed = (
        allowed
        & (query_index[:, None] - key_index[None, :] < WINDOW)
        & (key_doc[None, :] == query_doc[:, None])
    )
    scores = jnp.where(allowed[None, None], scores, -1e30)
    peak_score = jnp.max(scores, axis=-1, keepdims=True)
    raised = jnp.exp(scores - peak_score)
    weights = (raised / jnp.sum(raised, axis=-1, keepdims=True)).astype(jnp.bfloat16)
    layer_result = jnp.einsum(
        "grqk,kgd->qgrd", weights, value_rows, preferred_element_type=jnp.float32
    )
    return layer_result.astype(jnp.bfloat16).reshape(grouped_heads.shape[0], -1)


def local(x_in, norm_gain, w_query, w_key, value_projection, w_out, doc_ids):
    section_num = lax.axis_index("section")
    section_count = lax.axis_size("section")
    ctx_num = lax.axis_index("ctx")
    ctx_count = lax.axis_size("ctx")
    tp_count = lax.axis_size("tp")
    micro_count, half_rows, model_width = x_in.shape
    key_full, value_full, out_part = (
        lax.all_gather(w_key, "ctx", axis=1, tiled=True),
        lax.all_gather(value_projection, "ctx", axis=1, tiled=True),
        lax.all_gather(w_out, "ctx", axis=2, tiled=True),
    )
    query_weight = w_query[0]
    key_matrix = key_full[0]
    value_matrix = value_full[0]
    out_weight = out_part[0]
    tok_rows = half_rows * tp_count
    gain_row = norm_gain[0]
    query_heads = query_weight.shape[1] // HEAD_SIZE
    kv_heads = key_matrix.shape[1] // HEAD_SIZE
    group_size = query_heads // kv_heads
    reach_hops = min(-(-WINDOW // tok_rows), ctx_count - 1)
    token_index = ctx_num * tok_rows + jnp.arange(tok_rows, dtype=jnp.int32)
    key_index = (ctx_num - reach_hops) * tok_rows + jnp.arange(
        (reach_hops + 1) * tok_rows, dtype=jnp.int32
    )

    def project(operands):
        whole_rows, token_position = operands
        normalized_input = rms_normed(whole_rows, gain_row)
        query_matrix_rows = rotary_apply(
            jnp.dot(normalized_input, query_weight, preferred_element_type=jnp.float32).reshape(
                tok_rows, query_heads, HEAD_SIZE
            ),
            token_position,
        )
        key_matrix_rows = rotary_apply(
            jnp.dot(normalized_input, key_matrix, preferred_element_type=jnp.float32).reshape(
                tok_rows, kv_heads, HEAD_SIZE
            ),
            token_position,
        )
        value_rows = jnp.dot(
            normalized_input, value_matrix, preferred_element_type=jnp.float32
        ).astype(jnp.bfloat16)
        stacked = jnp.stack(
            [
                key_matrix_rows.astype(jnp.bfloat16).reshape(tok_rows, kv_heads * HEAD_SIZE),
                value_rows,
            ]
        )
        return (
            query_matrix_rows.astype(jnp.bfloat16).reshape(tok_rows, query_heads * HEAD_SIZE),
            stacked,
        )

    def skip_project(operands):
        return (
            jnp.zeros((tok_rows, query_heads * HEAD_SIZE), jnp.bfloat16),
            jnp.zeros((2, tok_rows, kv_heads * HEAD_SIZE), jnp.bfloat16),
        )

    def skip_attend(operands):
        return jnp.zeros((tok_rows, query_heads * HEAD_SIZE), jnp.bfloat16)

    def out_local(operands):
        return jnp.dot(operands, out_weight, preferred_element_type=jnp.float32)

    def skip_out(operands):
        return jnp.zeros((operands.shape[0], out_weight.shape[1]), jnp.float32)

    def step(step_num, carry):
        received, results = carry
        micro_num = step_num - section_num
        active = (micro_num >= 0) & (micro_num < micro_count)
        micro_at = jnp.clip(micro_num, 0, micro_count - 1)
        fresh_rows = lax.dynamic_index_in_dim(x_in, micro_at, 0, keepdims=False)
        current = jnp.where(section_num == 0, fresh_rows, received)
        whole_rows = lax.all_gather(current, "tp", axis=0, tiled=True)
        ids_row = lax.dynamic_index_in_dim(doc_ids, micro_at, 0, keepdims=False)
        token_position, query_doc = doc_lookup(ids_row, token_index, BLOCK)
        unused, key_doc = doc_lookup(ids_row, key_index, BLOCK)
        query_matrix_rows, stacked = lax.cond(
            active, project, skip_project, (whole_rows, token_position)
        )
        pieces = [shifted(stacked, "ctx", distance) for distance in range(reach_hops, 0, -1)]
        window_kv = jnp.concatenate(pieces + [stacked], axis=1)

        def attend(operands):
            query_part, window_part = operands
            grouped_heads = query_part.reshape(tok_rows, kv_heads, group_size, HEAD_SIZE)
            key_matrix_rows = window_part[0].reshape(-1, kv_heads, HEAD_SIZE)
            value_rows = window_part[1].reshape(-1, kv_heads, HEAD_SIZE)
            return attention_rows(
                grouped_heads,
                key_matrix_rows,
                value_rows,
                token_index,
                query_doc,
                key_index,
                key_doc,
            )

        attended = lax.cond(active, attend, skip_attend, (query_matrix_rows, window_kv))
        summed = lax.psum_scatter(
            lax.cond(active, out_local, skip_out, attended), "tp", scatter_dimension=0, tiled=True
        )
        updated = (current.astype(jnp.float32) + summed).astype(jnp.bfloat16)
        previous = lax.dynamic_index_in_dim(results, micro_at, 0, keepdims=False)
        results = lax.dynamic_update_index_in_dim(
            results, jnp.where(active, updated, previous), micro_at, 0
        )
        received = shifted(updated, "section", 1)
        return (received, results)

    start_carry = (
        jnp.zeros((half_rows, model_width), jnp.bfloat16),
        jnp.zeros((micro_count, half_rows, model_width), jnp.bfloat16),
    )
    unused_received, results = lax.fori_loop(0, micro_count + section_count - 1, step, start_carry)
    return results[None]


def solution(mesh):
    in_specs = (
        P(None, ("ctx", "tp"), None),
        P("section", None),
        P("section", None, "tp"),
        P("section", "ctx", "tp"),
        P("section", "ctx", "tp"),
        P("section", "tp", "ctx"),
        P(),
    )
    out_specs = P("section", None, ("ctx", "tp"), None)
    return jax.shard_map(local, mesh=mesh, in_specs=in_specs, out_specs=out_specs, check_vma=False)
```

profile of v0, /device:TPU:253, one launch (start us, length us, event | category | flops | bytes accessed | tf_op | source)
XLA Modules:
  0.0 1819.8 jit_solution(11641258674337430623)
XLA Ops:
  9.5 62.1 %all-gather.9.cloned.1.call-done = bf16[1,1024,2688]{1,2,0:T(8,128)(2,1)} async-done(((bf16[1,1024,168]{1,2,0:T(8,128)(2,1)}), bf16[1,1024,2688]{1,2,0:T(8,128)(2,1)}) %all-gather.9.cloned.1.call-update) | async-done | bytes 5505040 | tf_op jit(solution)/shard_map/all_gather | solution.py:93
  79.9 48.3 %all-gather.5.cloned.1.call-done = bf16[1,2688,512]{2,1,0:T(8,128)(2,1)} async-done(((bf16[1,168,512]{2,1,0:T(8,128)(2,1)}), bf16[1,2688,512]{2,1,0:T(8,128)(2,1)}) %all-gather.5.cloned.1.call-update) | async-done | bytes 2752528 | tf_op jit(solution)/shard_map/all_gather | solution.py:91
  128.2 56.1 %all-gather.7.cloned.1.call-done = bf16[1,2688,512]{2,1,0:T(8,128)(2,1)} async-done(((bf16[1,168,512]{2,1,0:T(8,128)(2,1)}), bf16[1,2688,512]{2,1,0:T(8,128)(2,1)}) %all-gather.7.cloned.1.call-update) | async-done | bytes 2752528 | tf_op jit(solution)/shard_map/all_gather | solution.py:92
  185.5 1627.5 %while.20 = (s32[]{:T(128)}, bf16[128,2688]{1,0:T(8,128)(2,1)S(1)}, bf16[2,128,2688]{2,1,0:T(8,128)(2,1)}, pred[]{:T(512)}, s32[]{:T(128)}, /*index=5*/bf16[2,12...) while((s32[]{:T(128)}, bf16[128,2688]{1,0:T(8,128)(2,1)S(1)}, ...), condition=%wide.region_15.16_spmd.clone.clone, body=%wide.region_0.15_spmd.clone.clone.sunk | while | flops 6283073536 | bytes 120011272 | solution.py:202
  188.0 30.7 %all-gather.11.cloned.1.call-done = bf16[256,2688]{1,0:T(8,128)(2,1)} async-done(((bf16[128,2688]{1,0:T(8,128)(2,1)}), bf16[256,2688]{1,0:T(8,128)(2,1)}) %all-gather.11.cloned.1.call-update) | async-done | bytes 1376272 | tf_op jit(solution)/shard_map/while/body/eval_jaxpr/all_gather | solution.py:161
  243.6 97.2 %reduce-scatter.2.cloned.1.call-done = f32[128,2688]{1,0:T(8,128)} async-done(((f32[256,2688]{1,0:T(8,128)}), f32[128,2688]{1,0:T(8,128)}) %reduce-scatter.2.cloned.1.call-update) | async-done | bytes 1376272 | tf_op jit(solution)/shard_map/while/body/eval_jaxpr/reduce_scatter | solution.py:187
  344.6 16.8 collective-permute-done.4
  363.7 33.0 %all-gather.11.cloned.1.call-done = bf16[256,2688]{1,0:T(8,128)(2,1)} async-done(((bf16[128,2688]{1,0:T(8,128)(2,1)}), bf16[256,2688]{1,0:T(8,128)(2,1)}) %all-gather.11.cloned.1.call-update) | async-done | bytes 1376272 | tf_op jit(solution)/shard_map/while/body/eval_jaxpr/all_gather | solution.py:161
  421.7 98.2 %reduce-scatter.2.cloned.1.call-done = f32[128,2688]{1,0:T(8,128)} async-done(((f32[256,2688]{1,0:T(8,128)}), f32[128,2688]{1,0:T(8,128)}) %reduce-scatter.2.cloned.1.call-update) | async-done | bytes 1376272 | tf_op jit(solution)/shard_map/while/body/eval_jaxpr/reduce_scatter | solution.py:187
  523.6 16.7 collective-permute-done.4
  542.7 33.4 %all-gather.11.cloned.1.call-done = bf16[256,2688]{1,0:T(8,128)(2,1)} async-done(((bf16[128,2688]{1,0:T(8,128)(2,1)}), bf16[256,2688]{1,0:T(8,128)(2,1)}) %all-gather.11.cloned.1.call-update) | async-done | bytes 1376272 | tf_op jit(solution)/shard_map/while/body/eval_jaxpr/all_gather | solution.py:161
  601.0 99.2 %reduce-scatter.2.cloned.1.call-done = f32[128,2688]{1,0:T(8,128)} async-done(((f32[256,2688]{1,0:T(8,128)}), f32[128,2688]{1,0:T(8,128)}) %reduce-scatter.2.cloned.1.call-update) | async-done | bytes 1376272 | tf_op jit(solution)/shard_map/while/body/eval_jaxpr/reduce_scatter | solution.py:187
  704.0 16.7 collective-permute-done.4
  723.0 33.1 %all-gather.11.cloned.1.call-done = bf16[256,2688]{1,0:T(8,128)(2,1)} async-done(((bf16[128,2688]{1,0:T(8,128)(2,1)}), bf16[256,2688]{1,0:T(8,128)(2,1)}) %all-gather.11.cloned.1.call-update) | async-done | bytes 1376272 | tf_op jit(solution)/shard_map/while/body/eval_jaxpr/all_gather | solution.py:161
  781.1 100.2 %reduce-scatter.2.cloned.1.call-done = f32[128,2688]{1,0:T(8,128)} async-done(((f32[256,2688]{1,0:T(8,128)}), f32[128,2688]{1,0:T(8,128)}) %reduce-scatter.2.cloned.1.call-update) | async-done | bytes 1376272 | tf_op jit(solution)/shard_map/while/body/eval_jaxpr/reduce_scatter | solution.py:187
  885.0 16.7 collective-permute-done.4
  904.1 33.1 %all-gather.11.cloned.1.call-done = bf16[256,2688]{1,0:T(8,128)(2,1)} async-done(((bf16[128,2688]{1,0:T(8,128)(2,1)}), bf16[256,2688]{1,0:T(8,128)(2,1)}) %all-gather.11.cloned.1.call-update) | async-done | bytes 1376272 | tf_op jit(solution)/shard_map/while/body/eval_jaxpr/all_gather | solution.py:161
  962.1 102.4 %reduce-scatter.2.cloned.1.call-done = f32[128,2688]{1,0:T(8,128)} async-done(((f32[256,2688]{1,0:T(8,128)}), f32[128,2688]{1,0:T(8,128)}) %reduce-scatter.2.cloned.1.call-update) | async-done | bytes 1376272 | tf_op jit(solution)/shard_map/while/body/eval_jaxpr/reduce_scatter | solution.py:187
  1068.2 16.7 collective-permute-done.4
  1087.3 33.1 %all-gather.11.cloned.1.call-done = bf16[256,2688]{1,0:T(8,128)(2,1)} async-done(((bf16[128,2688]{1,0:T(8,128)(2,1)}), bf16[256,2688]{1,0:T(8,128)(2,1)}) %all-gather.11.cloned.1.call-update) | async-done | bytes 1376272 | tf_op jit(solution)/shard_map/while/body/eval_jaxpr/all_gather | solution.py:161
  1145.3 102.4 %reduce-scatter.2.cloned.1.call-done = f32[128,2688]{1,0:T(8,128)} async-done(((f32[256,2688]{1,0:T(8,128)}), f32[128,2688]{1,0:T(8,128)}) %reduce-scatter.2.cloned.1.call-update) | async-done | bytes 1376272 | tf_op jit(solution)/shard_map/while/body/eval_jaxpr/reduce_scatter | solution.py:187
  1251.4 16.7 collective-permute-done.4
  1270.5 33.1 %all-gather.11.cloned.1.call-done = bf16[256,2688]{1,0:T(8,128)(2,1)} async-done(((bf16[128,2688]{1,0:T(8,128)(2,1)}), bf16[256,2688]{1,0:T(8,128)(2,1)}) %all-gather.11.cloned.1.call-update) | async-done | bytes 1376272 | tf_op jit(solution)/shard_map/while/body/eval_jaxpr/all_gather | solution.py:161
  1328.5 101.6 %reduce-scatter.2.cloned.1.call-done = f32[128,2688]{1,0:T(8,128)} async-done(((f32[256,2688]{1,0:T(8,128)}), f32[128,2688]{1,0:T(8,128)}) %reduce-scatter.2.cloned.1.call-update) | async-done | bytes 1376272 | tf_op jit(solution)/shard_map/while/body/eval_jaxpr/reduce_scatter | solution.py:187
  1433.8 16.7 collective-permute-done.4
  1452.9 33.1 %all-gather.11.cloned.1.call-done = bf16[256,2688]{1,0:T(8,128)(2,1)} async-done(((bf16[128,2688]{1,0:T(8,128)(2,1)}), bf16[256,2688]{1,0:T(8,128)(2,1)}) %all-gather.11.cloned.1.call-update) | async-done | bytes 1376272 | tf_op jit(solution)/shard_map/while/body/eval_jaxpr/all_gather | solution.py:161
  1523.1 17.6 conditional.13
  1547.7 64.0 %reduce-scatter.2.cloned.1.call-done = f32[128,2688]{1,0:T(8,128)} async-done(((f32[256,2688]{1,0:T(8,128)}), f32[128,2688]{1,0:T(8,128)}) %reduce-scatter.2.cloned.1.call-update) | async-done | bytes 1376272 | tf_op jit(solution)/shard_map/while/body/eval_jaxpr/reduce_scatter | solution.py:187
  1634.5 33.1 %all-gather.11.cloned.1.call-done = bf16[256,2688]{1,0:T(8,128)(2,1)} async-done(((bf16[128,2688]{1,0:T(8,128)(2,1)}), bf16[256,2688]{1,0:T(8,128)(2,1)}) %all-gather.11.cloned.1.call-update) | async-done | bytes 1376272 | tf_op jit(solution)/shard_map/while/body/eval_jaxpr/all_gather | solution.py:161
  1704.7 17.6 conditional.13
  1729.3 63.2 %reduce-scatter.2.cloned.1.call-done = f32[128,2688]{1,0:T(8,128)} async-done(((f32[256,2688]{1,0:T(8,128)}), f32[128,2688]{1,0:T(8,128)}) %reduce-scatter.2.cloned.1.call-update) | async-done | bytes 1376272 | tf_op jit(solution)/shard_map/while/body/eval_jaxpr/reduce_scatter | solution.py:187
  1796.2 16.8 collective-permute-done.4
  (455 shorter events, 428.5 us)
Async XLA Ops:
  6.5 65.0 %all-gather.9.cloned.1.call-start = ((), (), s32[]{:S(2)}) async-start(), calls=%async_computation.3 | async-start | bytes 5849088 | tf_op jit(solution)/shard_map/all_gather | solution.py:93
  7.3 121.0 %all-gather.5.cloned.1.call-start = ((), (), s32[]{:S(2)}) async-start(), calls=%async_computation.1 | async-start | bytes 2924544 | tf_op jit(solution)/shard_map/all_gather | solution.py:91
  8.0 176.3 %all-gather.7.cloned.1.call-start = ((), (), s32[]{:S(2)}) async-start(), calls=%async_computation.2 | async-start | bytes 2924544 | tf_op jit(solution)/shard_map/all_gather | solution.py:92
  185.5 33.1 %all-gather.11.cloned.1.call-start = ((), (), s32[]{:S(2)}) async-start(), calls=%async_computation.4 | async-start | bytes 2064384 | tf_op jit(solution)/shard_map/while/body/eval_jaxpr/all_gather | solution.py:161
  187.6 153.2 %reduce-scatter.2.cloned.1.call-start = ((), (), s32[]{:S(2)}) async-start(), calls=%async_computation.5 | async-start | bytes 4128768 | tf_op jit(solution)/shard_map/while/body/eval_jaxpr/reduce_scatter | solution.py:187
  222.3 17.3 collective-permute-start.2
  343.3 18.0 collective-permute-start.4
  361.3 35.4 %all-gather.11.cloned.1.call-start = ((), (), s32[]{:S(2)}) async-start(), calls=%async_computation.4 | async-start | bytes 2064384 | tf_op jit(solution)/shard_map/while/body/eval_jaxpr/all_gather | solution.py:161
  363.4 156.5 %reduce-scatter.2.cloned.1.call-start = ((), (), s32[]{:S(2)}) async-start(), calls=%async_computation.5 | async-start | bytes 4128768 | tf_op jit(solution)/shard_map/while/body/eval_jaxpr/reduce_scatter | solution.py:187
  400.3 17.3 collective-permute-start.2
  522.3 18.0 collective-permute-start.4
  540.3 35.8 %all-gather.11.cloned.1.call-start = ((), (), s32[]{:S(2)}) async-start(), calls=%async_computation.4 | async-start | bytes 2064384 | tf_op jit(solution)/shard_map/while/body/eval_jaxpr/all_gather | solution.py:161
  542.4 157.9 %reduce-scatter.2.cloned.1.call-start = ((), (), s32[]{:S(2)}) async-start(), calls=%async_computation.5 | async-start | bytes 4128768 | tf_op jit(solution)/shard_map/while/body/eval_jaxpr/reduce_scatter | solution.py:187
  702.7 18.0 collective-permute-start.4
  720.7 35.4 %all-gather.11.cloned.1.call-start = ((), (), s32[]{:S(2)}) async-start(), calls=%async_computation.4 | async-start | bytes 2064384 | tf_op jit(solution)/shard_map/while/body/eval_jaxpr/all_gather | solution.py:161
  722.7 158.5 %reduce-scatter.2.cloned.1.call-start = ((), (), s32[]{:S(2)}) async-start(), calls=%async_computation.5 | async-start | bytes 4128768 | tf_op jit(solution)/shard_map/while/body/eval_jaxpr/reduce_scatter | solution.py:187
  883.7 18.0 collective-permute-start.4
  901.7 35.4 %all-gather.11.cloned.1.call-start = ((), (), s32[]{:S(2)}) async-start(), calls=%async_computation.4 | async-start | bytes 2064384 | tf_op jit(solution)/shard_map/while/body/eval_jaxpr/all_gather | solution.py:161
  903.7 160.7 %reduce-scatter.2.cloned.1.call-start = ((), (), s32[]{:S(2)}) async-start(), calls=%async_computation.5 | async-start | bytes 4128768 | tf_op jit(solution)/shard_map/while/body/eval_jaxpr/reduce_scatter | solution.py:187
  1066.9 18.0 collective-permute-start.4
  1084.9 35.4 %all-gather.11.cloned.1.call-start = ((), (), s32[]{:S(2)}) async-start(), calls=%async_computation.4 | async-start | bytes 2064384 | tf_op jit(solution)/shard_map/while/body/eval_jaxpr/all_gather | solution.py:161
  1087.0 160.7 %reduce-scatter.2.cloned.1.call-start = ((), (), s32[]{:S(2)}) async-start(), calls=%async_computation.5 | async-start | bytes 4128768 | tf_op jit(solution)/shard_map/while/body/eval_jaxpr/reduce_scatter | solution.py:187
  1250.1 18.0 collective-permute-start.4
  1268.1 35.4 %all-gather.11.cloned.1.call-start = ((), (), s32[]{:S(2)}) async-start(), calls=%async_computation.4 | async-start | bytes 2064384 | tf_op jit(solution)/shard_map/while/body/eval_jaxpr/all_gather | solution.py:161
  1270.2 159.9 %reduce-scatter.2.cloned.1.call-start = ((), (), s32[]{:S(2)}) async-start(), calls=%async_computation.5 | async-start | bytes 4128768 | tf_op jit(solution)/shard_map/while/body/eval_jaxpr/reduce_scatter | solution.py:187
  1432.5 18.0 collective-permute-start.4
  1450.5 35.4 %all-gather.11.cloned.1.call-start = ((), (), s32[]{:S(2)}) async-start(), calls=%async_computation.4 | async-start | bytes 2064384 | tf_op jit(solution)/shard_map/while/body/eval_jaxpr/all_gather | solution.py:161
  1452.6 159.1 %reduce-scatter.2.cloned.1.call-start = ((), (), s32[]{:S(2)}) async-start(), calls=%async_computation.5 | async-start | bytes 4128768 | tf_op jit(solution)/shard_map/while/body/eval_jaxpr/reduce_scatter | solution.py:187
  1614.1 18.0 collective-permute-start.4
  1632.1 35.5 %all-gather.11.cloned.1.call-start = ((), (), s32[]{:S(2)}) async-start(), calls=%async_computation.4 | async-start | bytes 2064384 | tf_op jit(solution)/shard_map/while/body/eval_jaxpr/all_gather | solution.py:161
  1634.2 158.4 %reduce-scatter.2.cloned.1.call-start = ((), (), s32[]{:S(2)}) async-start(), calls=%async_computation.5 | async-start | bytes 4128768 | tf_op jit(solution)/shard_map/while/body/eval_jaxpr/reduce_scatter | solution.py:187
  1795.0 18.0 collective-permute-start.4
  (59 other events, 1550.0 us)
Sparse Core Ops, SparseCore 0:
  10.1 61.4 all-gather.8
  74.3 53.8 all-gather.4
  131.0 53.2 all-gather.6
  187.8 30.8 all-gather.10
  242.6 98.2 reduce-scatter.1
  363.6 33.0 all-gather.10
  420.6 99.2 reduce-scatter.1
  542.9 33.1 all-gather.10
  600.0 100.2 reduce-scatter.1
  723.0 33.1 all-gather.10
  780.0 101.1 reduce-scatter.1
  904.0 33.1 all-gather.10
  961.0 103.3 reduce-scatter.1
  1087.2 33.1 all-gather.10
  1144.2 103.3 reduce-scatter.1
  1270.4 33.1 all-gather.10
  1327.5 102.5 reduce-scatter.1
  1452.8 33.1 all-gather.10
  1546.6 65.0 reduce-scatter.1
  1634.4 33.1 all-gather.10
  1728.3 64.2 reduce-scatter.1
where the time goes:
time: 1830 us; the launch traced here: 1820 us
  waiting for transfers between devices  1580 us (86%)
  local copies, waits for them, and re-layouts  61.1 us (3%)
  starting transfers between devices  58.5 us (3%)
  other arithmetic  56.7 us (3%)
  matrix products  52.2 us (3%)
    reduce_scatter x9, waiting for transfers between devices, step(): lax.psum_scatter(lax.cond(active, out_local, skip_out, attended), 'tp', s...  829 us
    all_gather x9, waiting for transfers between devices, step(): whole_rows = lax.all_gather(current, 'tp', axis=0, tiled=True)  296 us
    ppermute x45, waiting for transfers between devices, shifted(): return lax.ppermute(shard, axis, pairs)  282 us
    all_gather x1, waiting for transfers between devices, local(): lax.all_gather(w_out, 'ctx', axis=2, tiled=True)  62.1 us
    ppermute x45, starting transfers between devices, shifted(): return lax.ppermute(shard, axis, pairs)  58 us
    all_gather x1, waiting for transfers between devices, local(): lax.all_gather(value_projection, 'ctx', axis=1, tiled=True)  56.1 us
    all_gather x1, waiting for transfers between devices, local(): lax.all_gather(w_key, 'ctx', axis=1, tiled=True)  48.3 us
  transfers between devices with their start and end apart: 66, of which 57 were waited for; matrix products, arithmetic and copies ran while one was open for 1% of the time, Pallas kernels for 0%

commit v1 on v0

v1 whole, which is shorter than its diff:
```python
import functools
import math

import jax
import jax.numpy as jnp
from jax import lax
from jax.experimental import pallas as pl
from jax.experimental.pallas import tpu as pltpu
from jax.sharding import PartitionSpec as P

HEAD = 128
WINDOW = 1024
BLOCK = 128
HALO = 5
CHUNK = 384
QUERY_SCALE = 168.0 ** (-0.5) * math.log2(math.e)
ROPE_BASE = 10000.0
MESH = pl.DeviceIdType.MESH


def dot32(a, b):
    return jnp.dot(a, b, preferred_element_type=jnp.float32)


def columns(j):
    return pl.ds(pl.multiple_of(j * CHUNK, 128), CHUNK)


def rope(rows, cosine, sine):
    return rows * cosine + pltpu.roll(rows, HEAD // 2, 1) * sine


def kernel(
    x_ref,
    gain_ref,
    wq_ref,
    wk_ref,
    wv_ref,
    wo_ref,
    cos_ref,
    sin_ref,
    bias_ref,
    out_ref,
    hid,
    hout,
    acc,
    squares,
    qbuf,
    kv,
    att,
    own,
    part_out,
    part_in,
    z_send,
    z_recv,
    g_send,
    g_recv,
    p_send,
    p_recv,
    k_send,
    k_recv,
    io_sem,
):
    section, ctx, tp = (lax.axis_index(a) for a in ("section", "ctx", "tp"))
    sections, ctxs = lax.axis_size("section"), lax.axis_size("ctx")
    micros, _, rows, width = hid.shape
    chunks = width // CHUNK
    odd = lax.rem(ctx, 2)
    even = odd == 0
    first, last = section == 0, section == sections - 1
    partner = {"tp": 1 - tp}
    core_mate = {"ctx": ctx + 1 - 2 * odd}

    def ctx_at(by):
        return {"ctx": lax.rem(ctx + by + ctxs, ctxs)}

    def section_at(by):
        return {"section": lax.rem(section + by + sections, sections)}

    def remote(src, dst, send, recv, to):
        return pltpu.make_async_remote_copy(
            src_ref=src, dst_ref=dst, send_sem=send, recv_sem=recv, device_id=to, device_id_type=MESH
        )

    for slot in range(HALO):

        @pl.when(2 * ctx + slot < HALO)
        def _():
            for m in range(micros):
                kv[m, slot] = jnp.zeros(kv.shape[2:], kv.dtype)

    barrier = pltpu.get_barrier_semaphore()
    greeted = [partner, core_mate, section_at(1), section_at(-1)]
    greeted += [ctx_at(by) for by in (2, -2, 3, -3)]
    for peer in greeted:
        pl.semaphore_signal(barrier, inc=1, device_id=peer, device_id_type=MESH)
    pl.semaphore_wait(barrier, len(greeted))

    def z_copy(m, j):
        c = columns(j)
        return remote(
            hout.at[m, :, c], hid.at[m, tp, :, c], z_send.at[m, j], z_recv.at[m, j], section_at(1)
        )

    def gather_copy(m, j):
        here = hid.at[m, tp, :, columns(j)]
        return remote(here, here, g_send.at[m, j], g_recv.at[m, j], partner)

    def part_copy(m, j):
        c = columns(j)
        return remote(
            part_out.at[m, :, c], part_in.at[m, :, c], p_send.at[m, j], p_recv.at[m, j], partner
        )

    def halo_two(m):
        return remote(
            kv.at[m, pl.ds(5, 2)], kv.at[m, pl.ds(1, 2)], k_send.at[m, 0], k_recv.at[m, 0], ctx_at(2)
        )

    def halo_three(m):
        return remote(kv.at[m, 6], kv.at[m, 0], k_send.at[m, 1], k_recv.at[m, 1], ctx_at(3))

    def halo_mate(m):
        return remote(
            kv.at[m, pl.ds(5, 2)], kv.at[m, pl.ds(3, 2)], k_send.at[m, 2], k_recv.at[m, 2], core_mate
        )

    def pass_pair(m):
        return remote(
            kv.at[m, pl.ds(1, 2)], kv.at[m, pl.ds(3, 2)], k_send.at[m, 2], k_recv.at[m, 2], core_mate
        )

    def pass_one(m):
        return remote(kv.at[m, 2], kv.at[m, 0], k_send.at[m, 1], k_recv.at[m, 1], core_mate)

    has_two = ctx >= 2
    sends_two = ctx < ctxs - 2
    sends_three = jnp.logical_and(odd == 1, ctx < ctxs - 3)
    passes_pair = jnp.logical_and(odd == 1, has_two)
    passes_one = jnp.logical_and(even, has_two)
    gets_pair = jnp.logical_or(odd == 1, has_two)
    gets_one = ctx >= 3

    def accumulate(m, j):
        c = columns(j)
        wide = hid[m, :, :, c].reshape(2 * rows, CHUNK).astype(jnp.float32)
        squares[...] += jnp.broadcast_to(
            jnp.sum(wide * wide, axis=1, keepdims=True), squares.shape
        )
        scaled = (wide * gain_ref[:, c].astype(jnp.float32)).astype(jnp.bfloat16)
        at = 0
        for weight in (wk_ref, wv_ref, wq_ref):
            for n in range(0, weight.shape[1], 512):
                acc[:, at : at + 512] += dot32(scaled, weight[c, n : n + 512])
                at += 512

    def micro(m, carry):
        acc[...] = jnp.zeros_like(acc)
        squares[...] = jnp.zeros_like(squares)

        @pl.when(first)
        def _():
            load = pltpu.make_async_copy(x_ref.at[m], hid.at[m, tp], io_sem)
            load.start()
            load.wait()

        def arrive(j, c):
            @pl.when(jnp.logical_not(first))
            def _():
                z_copy(m, j).wait_recv()

            gather_copy(m, j).start()

            @pl.when(j > 0)
            def _():
                gather_copy(m, j - 1).wait_recv()
                accumulate(m, j - 1)

            return c

        lax.fori_loop(0, chunks, arrive, 0)
        gather_copy(m, chunks - 1).wait_recv()
        accumulate(m, chunks - 1)

        scale = lax.rsqrt(squares[...] * (1.0 / width) + 1e-06)
        cosine, sine = cos_ref[m], sin_ref[m]
        kv_heads, query_heads = kv.shape[3], qbuf.shape[1]
        for h in range(kv_heads):
            key = rope(acc[:, h * HEAD : (h + 1) * HEAD] * scale, cosine, sine)
            at = (kv_heads + h) * HEAD
            value = acc[:, at : at + HEAD] * scale
            for t in range(2):
                kv[m, 5 + t, 0, h] = key[t * rows : (t + 1) * rows].astype(jnp.bfloat16)
                kv[m, 5 + t, 1, h] = value[t * rows : (t + 1) * rows].astype(jnp.bfloat16)

        @pl.when(sends_two)
        def _():
            halo_two(m).start()

        @pl.when(sends_three)
        def _():
            halo_three(m).start()

        @pl.when(even)
        def _():
            halo_mate(m).start()

        for h in range(query_heads):
            at = (2 * kv_heads + h) * HEAD
            query = rope(acc[:, at : at + HEAD] * (scale * QUERY_SCALE), cosine, sine)
            for t in range(2):
                qbuf[t, h] = query[t * rows : (t + 1) * rows].astype(jnp.bfloat16)

        @pl.when(has_two)
        def _():
            halo_two(m).wait_recv()

        @pl.when(passes_pair)
        def _():
            pass_pair(m).start()

        @pl.when(passes_one)
        def _():
            pass_one(m).start()

        @pl.when(gets_one)
        def _():
            halo_three(m).wait_recv()

        @pl.when(gets_pair)
        def _():
            halo_mate(m).wait_recv()

        group = query_heads // kv_heads

        def attend(i, c):
            t, g = i // kv_heads, lax.rem(i, kv_heads)
            query = qbuf[t, pl.ds(g * group, group)].reshape(group * rows, HEAD)
            key = kv[m, pl.ds(t, HALO + 1), 0, g].reshape((HALO + 1) * rows, HEAD)
            value = kv[m, pl.ds(t, HALO + 1), 1, g].reshape((HALO + 1) * rows, HEAD)
            scores = lax.dot_general(
                query, key, (((1,), (1,)), ((), ())), preferred_element_type=jnp.float32
            )
            bias = bias_ref[m, t]
            for r in range(group):
                own_scores = scores[r * rows : (r + 1) * rows] + bias
                peak = jnp.max(own_scores, axis=1, keepdims=True)
                raised = jnp.exp2(own_scores - peak)
                total = jnp.sum(raised, axis=1, keepdims=True)
                mixed = dot32(raised.astype(jnp.bfloat16), value) / total
                att[t, g, :, r * HEAD : (r + 1) * HEAD] = mixed.astype(jnp.bfloat16)
            return c

        lax.fori_loop(0, 2 * kv_heads, attend, 0)

        def project(j, c):
            cols = columns(j)
            total = jnp.zeros((2 * rows, CHUNK), jnp.float32)
            for g in range(kv_heads):
                depth = group * HEAD
                total += dot32(
                    att[:, g].reshape(2 * rows, depth), wo_ref[g * depth : (g + 1) * depth, cols]
                )
            top, bottom = total[:rows], total[rows:]
            part_out[m, :, cols] = jnp.where(tp == 0, bottom, top).astype(jnp.bfloat16)
            part_copy(m, j).start()
            own[:, cols] = jnp.where(tp == 0, top, bottom) + hid[m, tp, :, cols].astype(jnp.float32)
            return c

        lax.fori_loop(0, chunks, project, 0)

        def finish(j, c):
            cols = columns(j)
            part_copy(m, j).wait_recv()
            hout[m, :, cols] = (own[:, cols] + part_in[m, :, cols].astype(jnp.float32)).astype(
                jnp.bfloat16
            )

            @pl.when(jnp.logical_not(last))
            def _():
                z_copy(m, j).start()

            return c

        lax.fori_loop(0, chunks, finish, 0)
        pltpu.make_async_copy(hout.at[m], out_ref.at[0, m], io_sem).start()
        pltpu.make_async_copy(hout.at[m], out_ref.at[0, m], io_sem).wait()
        return carry

    lax.fori_loop(0, micros, micro, 0)

    def drain(m, carry):
        def one(j, c):
            gather_copy(m, j).wait_send()
            part_copy(m, j).wait_send()

            @pl.when(jnp.logical_not(last))
            def _():
                z_copy(m, j).wait_send()

            return c

        lax.fori_loop(0, chunks, one, 0)

        @pl.when(sends_two)
        def _():
            halo_two(m).wait_send()

        @pl.when(sends_three)
        def _():
            halo_three(m).wait_send()

        @pl.when(passes_one)
        def _():
            pass_one(m).wait_send()

        @pl.when(even)
        def _():
            halo_mate(m).wait_send()

        @pl.when(passes_pair)
        def _():
            pass_pair(m).wait_send()

        return carry

    lax.fori_loop(0, micros, drain, 0)


def doc_lookup(ids, token_index):
    blocks = ids.shape[1]
    start = jnp.sum((ids[:, None, :] < ids[:, :, None]).astype(jnp.int32), axis=2)
    block_of = jnp.clip(token_index // BLOCK, 0, blocks - 1)
    onehot = (block_of[:, None] == jnp.arange(blocks, dtype=jnp.int32)[None, :]).astype(jnp.int32)
    start_of = jnp.sum(onehot[None] * start[:, None, :], axis=2)
    doc_of = jnp.sum(onehot[None] * ids[:, None, :], axis=2)
    return token_index[None] - start_of * BLOCK, doc_of


def tables(doc_ids, rows):
    ctx = lax.axis_index("ctx")
    token_index = ctx * 2 * rows + jnp.arange(2 * rows, dtype=jnp.int32)
    position, query_doc = doc_lookup(doc_ids, token_index)
    frequency = ROPE_BASE ** (-(jnp.arange(HEAD // 2, dtype=jnp.float32) * 2.0) / HEAD)
    angles = position.astype(jnp.float32)[:, :, None] * frequency
    cosine, sine = jnp.cos(angles), jnp.sin(angles)
    key_index = (2 * ctx - HALO) * rows + jnp.arange((HALO + 2) * rows, dtype=jnp.int32)
    unused, key_doc = doc_lookup(doc_ids, key_index)
    biases = []
    for t in range(2):
        q_at = token_index[t * rows : (t + 1) * rows][:, None]
        k_at = key_index[t * rows : (t + HALO + 1) * rows][None, :]
        q_doc = query_doc[:, t * rows : (t + 1) * rows, None]
        k_doc = key_doc[:, None, t * rows : (t + HALO + 1) * rows]
        allowed = (k_at >= 0) & (k_at <= q_at) & (q_at - k_at < WINDOW)
        biases.append(jnp.where(allowed[None] & (q_doc == k_doc), 0.0, -1e30))
    return (
        jnp.concatenate([cosine, cosine], axis=-1),
        jnp.concatenate([-sine, sine], axis=-1),
        jnp.stack(biases, axis=1).astype(jnp.float32),
    )


def local(x_in, norm_gain, w_query, w_key, value_projection, w_out, doc_ids):
    micros, rows, width = x_in.shape
    wq = w_query[0]
    wk = lax.all_gather(w_key, "ctx", axis=1, tiled=True)[0]
    wv = lax.all_gather(value_projection, "ctx", axis=1, tiled=True)[0]
    wo = lax.all_gather(w_out, "ctx", axis=2, tiled=True)[0]
    cosine, sine, bias = tables(doc_ids, rows)
    query_heads, kv_heads = wq.shape[1] // HEAD, wk.shape[1] // HEAD
    chunks = width // CHUNK
    vmem = pl.BlockSpec(memory_space=pltpu.VMEM)
    hbm = pl.BlockSpec(memory_space=pl.ANY)
    per_chunk = pltpu.SemaphoreType.DMA((micros, chunks))
    return pl.pallas_call(
        kernel,
        out_shape=jax.ShapeDtypeStruct((1, micros, rows, width), jnp.bfloat16),
        in_specs=[hbm] + [vmem] * 8,
        out_specs=hbm,
        scratch_shapes=[
            pltpu.VMEM((micros, 2, rows, width), jnp.bfloat16),
            pltpu.VMEM((micros, rows, width), jnp.bfloat16),
            pltpu.VMEM((2 * rows, (query_heads + 2 * kv_heads) * HEAD), jnp.float32),
            pltpu.VMEM((2 * rows, HEAD), jnp.float32),
            pltpu.VMEM((2, query_heads, rows, HEAD), jnp.bfloat16),
            pltpu.VMEM((micros, HALO + 2, 2, kv_heads, rows, HEAD), jnp.bfloat16),
            pltpu.VMEM((2, kv_heads, rows, query_heads // kv_heads * HEAD), jnp.bfloat16),
            pltpu.VMEM((rows, width), jnp.float32),
            pltpu.VMEM((micros, rows, width), jnp.bfloat16),
            pltpu.VMEM((micros, rows, width), jnp.bfloat16),
        ]
        + [per_chunk] * 6
        + [
            pltpu.SemaphoreType.DMA((micros, 3)),
            pltpu.SemaphoreType.DMA((micros, 3)),
            pltpu.SemaphoreType.DMA,
        ],
        compiler_params=pltpu.CompilerParams(
            collective_id=0, has_side_effects=True, vmem_limit_bytes=60 * 1024 * 1024
        ),
    )(x_in, norm_gain, wq, wk, wv, wo, cosine, sine, bias)


def solution(mesh):
    in_specs = (
        P(None, ("ctx", "tp"), None),
        P("section", None),
        P("section", None, "tp"),
        P("section", "ctx", "tp"),
        P("section", "ctx", "tp"),
        P("section", "tp", "ctx"),
        P(),
    )
    out_specs = P("section", None, ("ctx", "tp"), None)
    return jax.shard_map(local, mesh=mesh, in_specs=in_specs, out_specs=out_specs, check_vma=False)
```

time: 1830 us -> 628 us (0.34)
  waiting for transfers between devices: 1580 us -> 162 us
  Pallas kernels: 0 us -> 434 us
  starting transfers between devices: 58.5 us -> 0.08 us
  matrix products: 52.2 us -> 0 us
  local copies, waits for them, and re-layouts: 61.1 us -> 10.5 us
  other arithmetic: 56.7 us -> 7.32 us
    reduce_scatter x9 -> x0, waiting for transfers between devices: 829 us -> none  [step(): lax.psum_scatter(lax.cond(active, out_local, skip_out, attended), 'tp', s...]
    pallas_call x0 -> x1, Pallas kernels: none -> 434 us  [local(): pl.pallas_call(kernel, out_shape=jax.ShapeDtypeStruct((1, micros, rows, w...]
    all_gather x12 -> x3, waiting for transfers between devices: 462 us -> 160 us  [the longest x1 56.1 us: local(): wv = lax.all_gather(value_projection, 'ctx', axis=1, tiled=True)[0]]
    ppermute x45 -> x0, waiting for transfers between devices: 282 us -> none  [shifted(): return lax.ppermute(shard, axis, pairs)]
    ppermute x45 -> x0, starting transfers between devices: 58 us -> none  [shifted(): return lax.ppermute(shard, axis, pairs)]
    dot_general x10 -> x0, matrix products: 42 us -> none  [the longest x2 13.2 us: attention_rows(): jnp.einsum('grqk,kgd->qgrd', weights, value_rows, preferred_element_type=...]
    dynamic_update_slice x9 -> x0, other arithmetic: 21.7 us -> none  [step(): lax.dynamic_update_index_in_dim(results, jnp.where(active, updated, previ...]
  transfers between devices with their start and end apart: 66 -> 3, of which waited for: 57 -> 3; matrix products, arithmetic and copies ran while one was open for 1% -> 2% of each run, Pallas kernels for 0% -> 0%
where the time goes in v1:
time: 628 us; the launch traced here: 627 us
  Pallas kernels  434 us (69%)
  waiting for transfers between devices  162 us (26%)
  between operations  13.2 us (2%)
  local copies, waits for them, and re-layouts  10.5 us (2%)
  other arithmetic  7.32 us (1%)
    pallas_call x1, Pallas kernels, local(): pl.pallas_call(kernel, out_shape=jax.ShapeDtypeStruct((1, micros, rows, w...  434 us
    all_gather x1, waiting for transfers between devices, local(): wv = lax.all_gather(value_projection, 'ctx', axis=1, tiled=True)[0]  56.1 us
    all_gather x1, waiting for transfers between devices, local(): wo = lax.all_gather(w_out, 'ctx', axis=2, tiled=True)[0]  55.4 us
    all_gather x1, waiting for transfers between devices, local(): wk = lax.all_gather(w_key, 'ctx', axis=1, tiled=True)[0]  48.7 us
  transfers between devices with their start and end apart: 3, of which 3 were waited for; matrix products, arithmetic and copies ran while one was open for 2% of the time, Pallas kernels for 0%

profile of v1, /device:TPU:253, one launch (start us, length us, event | category | flops | bytes accessed | tf_op | source)
XLA Modules:
  0.0 627.2 jit_solution(8126339746833114637)
XLA Ops:
  6.5 0.0 all-gather.8.cloned.1.call-start
  6.5 0.7 all-gather.8.cloned.1.call-update
  7.3 0.0 all-gather.4.cloned.1.call-start
  7.3 0.7 all-gather.4.cloned.1.call-update
  8.0 0.0 all-gather.6.cloned.1.call-start
  8.1 0.7 all-gather.6.cloned.1.call-update
  8.8 0.9 convert_reduce_fusion
  9.7 0.8 multiply_reduce_fusion.1
  10.5 0.8 multiply_reduce_fusion
  11.4 1.0 fusion.3
  12.3 0.8 pad_maximum_fusion.1.cos_ref
  13.2 0.8 pad_maximum_fusion.2.sin_ref
  14.1 0.2 fusion.1
  14.3 0.2 fusion
  14.5 0.2 and_select_fusion
  14.7 0.2 and_select_fusion.1
  14.9 1.3 pad_maximum_fusion.bias_ref
  16.2 55.4 %all-gather.8.cloned.1.call-done = bf16[1,1024,2688]{1,2,0:T(8,128)(2,1)} async-done(((bf16[1,1024,168]{1,2,0:T(8,128)(2,1)}), bf16[1,1024,2688]{1,2,0:T(8,128)(2,1)}) %all-gather.8.cloned.1.call-update) | async-done | bytes 5505040 | tf_op jit(solution)/shard_map/all_gather | solution.py:369
  71.6 7.9 %copy.10 = bf16[1,1024,2688]{2,1,0:T(8,128)(2,1)} copy(bf16[1,1024,2688]{1,2,0:T(8,128)(2,1)} %all-gather.8.cloned.1.call-done) | data formatting | bytes 11010048 | tf_op jit(solution)/shard_map/all_gather | solution.py:369
  79.5 48.7 %all-gather.4.cloned.1.call-done = bf16[1,2688,512]{2,1,0:T(8,128)(2,1)} async-done(((bf16[1,168,512]{2,1,0:T(8,128)(2,1)}), bf16[1,2688,512]{2,1,0:T(8,128)(2,1)}) %all-gather.4.cloned.1.call-update) | async-done | bytes 2752528 | tf_op jit(solution)/shard_map/all_gather | solution.py:367
  128.2 56.1 %all-gather.6.cloned.1.call-done = bf16[1,2688,512]{2,1,0:T(8,128)(2,1)} async-done(((bf16[1,168,512]{2,1,0:T(8,128)(2,1)}), bf16[1,2688,512]{2,1,0:T(8,128)(2,1)}) %all-gather.6.cloned.1.call-update) | async-done | bytes 2752528 | tf_op jit(solution)/shard_map/all_gather | solution.py:368
  184.3 433.8 %shard_map.73 = bf16[1,2,128,2688]{3,2,1,0:T(8,128)(2,1)} custom-call(bf16[2,128,2688]{2,1,0:T(8,128)(2,1)} %x_ref.1, bf16[1,2688]{1,0:T(2,128)(2,1)} %gain_ref.1, bf16[2688,1024]{1,0:T(8,128)(2,1)} %bitcast.5, bf16[2688,512]{1,0:T(8,128)(2,1)} %bitcast.6, bf16[2688,512]{1,0:T(8,128)(2,1)} %bitcast.7, bf16[1024,2688]{1,0:T(8,128)(2,1)} %bitcast.4, ...), custom_call_target="tpu_custom_call" | custom-call | tf_op jit(solution)/shard_map/pallas_call | solution.py:376
  618.1 2.5 copy.12
  (11 shorter events, 0.1 us)
Async XLA Ops:
  6.5 65.0 %all-gather.8.cloned.1.call-start = ((), (), s32[]{:S(2)}) async-start(), calls=%async_computation.2 | async-start | bytes 5849088 | tf_op jit(solution)/shard_map/all_gather | solution.py:369
  7.3 121.0 %all-gather.4.cloned.1.call-start = ((), (), s32[]{:S(2)}) async-start(), calls=%async_computation | async-start | bytes 2924544 | tf_op jit(solution)/shard_map/all_gather | solution.py:367
  8.0 176.3 %all-gather.6.cloned.1.call-start = ((), (), s32[]{:S(2)}) async-start(), calls=%async_computation.1 | async-start | bytes 2924544 | tf_op jit(solution)/shard_map/all_gather | solution.py:368
Sparse Core Ops, SparseCore 0:
  10.1 61.4 all-gather.7
  74.3 53.8 all-gather.3
  131.0 53.2 all-gather.5

commit v2 on v1

v2 whole, which is shorter than its diff:
```python
import functools
import math

import jax
import jax.numpy as jnp
from jax import lax
from jax.experimental import pallas as pl
from jax.experimental.pallas import tpu as pltpu
from jax.sharding import PartitionSpec as P

HEAD = 128
WINDOW = 1024
BLOCK = 128
HALO = 5
CHUNK = 384
PIECE = 128
QUERY_SCALE = 168.0 ** (-0.5) * math.log2(math.e)
ROPE_BASE = 10000.0
MESH = pl.DeviceIdType.MESH


def dot32(a, b):
    return jnp.dot(a, b, preferred_element_type=jnp.float32)


def columns(j):
    return pl.ds(pl.multiple_of(j * CHUNK, 128), CHUNK)


def rope(rows, cosine, sine):
    return rows * cosine + pltpu.roll(rows, HEAD // 2, 1) * sine


def kernel(
    x_ref,
    gain_ref,
    wq_ref,
    wk_ref,
    wv_ref,
    wo_ref,
    cos_ref,
    sin_ref,
    bias_ref,
    out_ref,
    wq,
    kv_parts,
    o_parts,
    wkv,
    wo,
    hid,
    hout,
    acc,
    squares,
    qbuf,
    kv,
    att,
    own,
    part_out,
    part_in,
    z_send,
    z_recv,
    g_send,
    g_recv,
    p_send,
    p_recv,
    k_send,
    k_recv,
    w_send,
    w_recv,
    load_sem,
    io_sem,
):
    section, ctx, tp = (lax.axis_index(a) for a in ("section", "ctx", "tp"))
    sections, ctxs = lax.axis_size("section"), lax.axis_size("ctx")
    micros, _, rows, width = hid.shape
    chunks, per_chunk = width // CHUNK, CHUNK // PIECE
    kv_heads, query_heads = kv.shape[1], qbuf.shape[1]
    group = query_heads // kv_heads
    odd = lax.rem(ctx, 2)
    even = odd == 0
    first, last = section == 0, section == sections - 1
    partner = {"tp": 1 - tp}
    mate = ctx + 1 - 2 * odd
    core_mate = {"ctx": mate}

    def wrap(index):
        return lax.rem(index + ctxs, ctxs)

    def ctx_at(by):
        return {"ctx": wrap(ctx + by)}

    def section_at(by):
        return {"section": lax.rem(section + by + sections, sections)}

    def remote(src, dst, send, recv, to):
        return pltpu.make_async_remote_copy(
            src_ref=src, dst_ref=dst, send_sem=send, recv_sem=recv, device_id=to, device_id_type=MESH
        )

    half = wo_ref.shape[1] // 2
    loads = [
        pltpu.make_async_copy(wk_ref.at[0], kv_parts.at[0, ctx], load_sem.at[0]),
        pltpu.make_async_copy(wv_ref.at[0], kv_parts.at[1, ctx], load_sem.at[1]),
        pltpu.make_async_copy(wo_ref.at[0, pl.ds(0, half)], o_parts.at[0, ctx], load_sem.at[2]),
        pltpu.make_async_copy(wo_ref.at[0, pl.ds(half, half)], o_parts.at[1, ctx], load_sem.at[3]),
        pltpu.make_async_copy(wq_ref.at[0], wq, load_sem.at[4]),
    ]
    for load in loads:
        load.start()

    def x_load(m):
        return pltpu.make_async_copy(x_ref.at[m], hid.at[m, tp], io_sem.at[m])

    @pl.when(first)
    def _():
        for m in range(micros):
            x_load(m).start()

    for slot in range(HALO):

        @pl.when(2 * ctx + slot < HALO)
        def _():
            for m in range(micros):
                for g in range(kv_heads):
                    kv[m, g, slot] = jnp.zeros(kv.shape[3:], kv.dtype)

    barrier = pltpu.get_barrier_semaphore()
    greeted = [partner, core_mate, section_at(1), section_at(-1)]
    greeted += [ctx_at(by) for by in (2, -2, 3, -3, 4, -4)]
    for peer in greeted:
        pl.semaphore_signal(barrier, inc=1, device_id=peer, device_id_type=MESH)
    pl.semaphore_wait(barrier, len(greeted))

    def piece(j):
        return pl.ds(pl.multiple_of(j * PIECE, PIECE), PIECE)

    def z_copy(m, j):
        c = piece(j)
        return remote(
            hout.at[m, :, c], hid.at[m, tp, :, c], z_send.at[m, j], z_recv.at[m, j], section_at(1)
        )

    def gather_copy(m, j):
        here = hid.at[m, tp, :, piece(j)]
        return remote(here, here, g_send.at[m, j], g_recv.at[m, j], partner)

    def part_copy(m, j):
        c = piece(j)
        return remote(
            part_out.at[m, :, c], part_in.at[m, :, c], p_send.at[m, j], p_recv.at[m, j], partner
        )

    def halo(m, g, n, src, dst, to):
        return remote(
            kv.at[m, g, src], kv.at[m, g, dst], k_send.at[m, n, g], k_recv.at[m, n, g], to
        )

    def halo_two(m, g):
        return halo(m, g, 0, pl.ds(5, 2), pl.ds(1, 2), ctx_at(2))

    def halo_three(m, g):
        return halo(m, g, 1, 6, 0, ctx_at(3))

    def halo_mate(m, g):
        return halo(m, g, 2, pl.ds(5, 2), pl.ds(3, 2), core_mate)

    def pass_pair(m, g):
        return halo(m, g, 2, pl.ds(1, 2), pl.ds(3, 2), core_mate)

    def pass_one(m, g):
        return halo(m, g, 1, 2, 0, core_mate)

    has_two = ctx >= 2
    sends_two = ctx < ctxs - 2
    sends_three = jnp.logical_and(odd == 1, ctx < ctxs - 3)
    passes_pair = jnp.logical_and(odd == 1, has_two)
    passes_one = jnp.logical_and(even, has_two)
    gets_pair = jnp.logical_or(odd == 1, has_two)
    gets_one = ctx >= 3

    across = ctx + 2 - 4 * lax.rem(ctx // 2, 2)
    stream = [wrap(at + by) for by in (0, -4, 4, 8) for at in (ctx, across)]
    mine, beside, up, up_beside, down, down_beside, far, far_beside = stream
    to_across, to_down, to_up = {"ctx": across}, ctx_at(4), ctx_at(-4)

    def w_copy(kind, p, slot, n, to):
        ref = (kv_parts, o_parts)[kind].at[p, slot]
        k = 2 * kind + p
        return remote(ref, ref, w_send.at[k, n], w_recv.at[k, slot], to)

    def w_wait(kind, p, slot):
        w_copy(kind, p, slot, 0, core_mate).wait_recv()

    def w_own(kind):
        for p in range(2):
            for n, to in enumerate((to_across, to_down, to_up, core_mate)):
                w_copy(kind, p, mine, n, to).start()

    def w_beside(kind):
        for p in range(2):
            w_wait(kind, p, beside)
            for n, to in enumerate((to_down, to_up, core_mate)):
                w_copy(kind, p, beside, 4 + n, to).start()

    def w_onward(kind):
        for p, onward in enumerate((to_down, to_up)):
            for n, slot in enumerate(((up, up_beside), (down, down_beside))[p]):
                w_wait(kind, p, slot)
                w_copy(kind, p, slot, 7 + n, onward).start()
                w_copy(kind, p, slot, 9 + n, core_mate).start()
        for p in range(2):
            for n, slot in enumerate(((down, down_beside), (up, up_beside))[p]):
                w_wait(kind, p, slot)
                w_copy(kind, p, slot, 11 + n, core_mate).start()

    def w_last(kind):
        for p in range(2):
            for n, slot in enumerate((far, far_beside)):
                w_wait(kind, p, slot)
                w_copy(kind, p, slot, 13 + n, core_mate).start()
        for p in range(2):
            for slot in stream:
                w_wait(kind, p, slot + 1 - 2 * odd)

    def w_drain(kind):
        for p in range(2):
            for n in range(15):
                w_copy(kind, p, mine, n, core_mate).wait_send()

    deep = kv_parts.shape[2]

    def assemble_kv():
        for p in range(2):
            for i in range(kv_parts.shape[1]):
                wkv[p, i * deep : (i + 1) * deep, :] = kv_parts[p, i]

    def assemble_o():
        step = 32

        def some(r, c):
            for p in range(2):
                at = pl.ds(pl.multiple_of(r * step, step), step)
                to = pl.ds(pl.multiple_of(p * half + r * step, step), step)
                for i in range(o_parts.shape[1]):
                    wo[to, i * deep : (i + 1) * deep] = o_parts[p, i, at, :]
            return c

        lax.fori_loop(0, half // step, some, 0)

    for load in loads[:4]:
        load.wait()
    w_own(0)

    @pl.when(first)
    def _():
        for m in range(micros):
            x_load(m).wait()

        def spread(i, c):
            gather_copy(i // (chunks * per_chunk), lax.rem(i, chunks * per_chunk)).start()
            return c

        lax.fori_loop(0, micros * chunks * per_chunk, spread, 0)

    w_beside(0)
    w_onward(0)
    w_last(0)
    w_own(1)
    assemble_kv()

    @pl.when(jnp.logical_not(first))
    def _():
        w_beside(1)
        w_onward(1)
        w_last(1)
        assemble_o()

    loads[4].wait()

    def accumulate(m, j):
        c = columns(j)
        wide = hid[m, :, :, c].reshape(2 * rows, CHUNK).astype(jnp.float32)
        squares[...] += jnp.broadcast_to(
            jnp.sum(wide * wide, axis=1, keepdims=True), squares.shape
        )
        scaled = (wide * gain_ref[:, c].astype(jnp.float32)).astype(jnp.bfloat16)
        at = 0
        for weight in (wkv.at[0], wkv.at[1], wq):
            for n in range(0, weight.shape[1], 512):
                acc[:, at : at + 512] += dot32(scaled, weight[c, n : n + 512])
                at += 512

    def micro(m, carry):
        acc[...] = jnp.zeros_like(acc)
        squares[...] = jnp.zeros_like(squares)
        starts = jnp.logical_and(first, m == 0)

        def gathered(j):
            for i in range(per_chunk):
                gather_copy(m, j * per_chunk + i).wait_recv()

        def arrive(j, c):
            @pl.when(jnp.logical_not(first))
            def _():
                for i in range(per_chunk):
                    z_copy(m, j * per_chunk + i).wait_recv()
                    gather_copy(m, j * per_chunk + i).start()

            @pl.when(j > 0)
            def _():
                gathered(j - 1)
                accumulate(m, j - 1)

            return c

        lax.fori_loop(0, chunks, arrive, 0)
        gathered(chunks - 1)
        accumulate(m, chunks - 1)

        @pl.when(starts)
        def _():
            w_beside(1)

        scale = lax.rsqrt(squares[...] * (1.0 / width) + 1e-06)
        cosine, sine = cos_ref[m], sin_ref[m]
        for h in range(kv_heads):
            key = rope(acc[:, h * HEAD : (h + 1) * HEAD] * scale, cosine, sine)
            at = (kv_heads + h) * HEAD
            value = acc[:, at : at + HEAD] * scale
            for t in range(2):
                kv[m, h, 5 + t, 0] = key[t * rows : (t + 1) * rows].astype(jnp.bfloat16)
                kv[m, h, 5 + t, 1] = value[t * rows : (t + 1) * rows].astype(jnp.bfloat16)

            @pl.when(sends_two)
            def _():
                halo_two(m, h).start()

            @pl.when(sends_three)
            def _():
                halo_three(m, h).start()

            @pl.when(even)
            def _():
                halo_mate(m, h).start()

        for h in range(query_heads):
            at = (2 * kv_heads + h) * HEAD
            query = rope(acc[:, at : at + HEAD] * (scale * QUERY_SCALE), cosine, sine)
            for t in range(2):
                qbuf[t, h] = query[t * rows : (t + 1) * rows].astype(jnp.bfloat16)

        def relay(g):
            @pl.when(has_two)
            def _():
                halo_two(m, g).wait_recv()

            @pl.when(passes_pair)
            def _():
                pass_pair(m, g).start()

            @pl.when(passes_one)
            def _():
                pass_one(m, g).start()

        def attend(g, c):
            @pl.when(g < kv_heads - 1)
            def _():
                relay(g + 1)

            @pl.when(gets_one)
            def _():
                halo_three(m, g).wait_recv()

            @pl.when(gets_pair)
            def _():
                halo_mate(m, g).wait_recv()

            for t in range(2):
                query = qbuf[t, pl.ds(g * group, group)].reshape(group * rows, HEAD)
                key = kv[m, g, t : t + HALO + 1, 0].reshape((HALO + 1) * rows, HEAD)
                value = kv[m, g, t : t + HALO + 1, 1].reshape((HALO + 1) * rows, HEAD)
                scores = lax.dot_general(
                    query, key, (((1,), (1,)), ((), ())), preferred_element_type=jnp.float32
                )
                bias = bias_ref[m, t]
                for r in range(group):
                    own_scores = scores[r * rows : (r + 1) * rows] + bias
                    peak = jnp.max(own_scores, axis=1, keepdims=True)
                    raised = jnp.exp2(own_scores - peak)
                    total = jnp.sum(raised, axis=1, keepdims=True)
                    mixed = dot32(raised.astype(jnp.bfloat16), value) / total
                    att[t, g, :, r * HEAD : (r + 1) * HEAD] = mixed.astype(jnp.bfloat16)

            @pl.when(jnp.logical_and(starts, g == 0))
            def _():
                w_onward(1)

            return c

        relay(0)
        lax.fori_loop(0, kv_heads, attend, 0)

        @pl.when(starts)
        def _():
            w_last(1)
            assemble_o()

        def project(j, c):
            cols = columns(j)
            total = jnp.zeros((2 * rows, CHUNK), jnp.float32)
            for g in range(kv_heads):
                depth = group * HEAD
                total += dot32(
                    att[:, g].reshape(2 * rows, depth), wo[g * depth : (g + 1) * depth, cols]
                )
            top, bottom = total[:rows], total[rows:]
            part_out[m, :, cols] = jnp.where(tp == 0, bottom, top).astype(jnp.bfloat16)
            for i in range(per_chunk):
                part_copy(m, j * per_chunk + i).start()
            own[:, cols] = jnp.where(tp == 0, top, bottom) + hid[m, tp, :, cols].astype(jnp.float32)
            return c

        lax.fori_loop(0, chunks, project, 0)

        def finish(j, c):
            cols = piece(j)
            part_copy(m, j).wait_recv()
            hout[m, :, cols] = (own[:, cols] + part_in[m, :, cols].astype(jnp.float32)).astype(
                jnp.bfloat16
            )

            @pl.when(jnp.logical_not(last))
            def _():
                z_copy(m, j).start()

            return c

        lax.fori_loop(0, chunks * per_chunk, finish, 0)
        pltpu.make_async_copy(hout.at[m], out_ref.at[0, m], io_sem.at[m]).start()
        return carry

    lax.fori_loop(0, micros, micro, 0)

    w_drain(0)
    w_drain(1)

    def drain(m, carry):
        pltpu.make_async_copy(hout.at[m], out_ref.at[0, m], io_sem.at[m]).wait()

        def one(j, c):
            gather_copy(m, j).wait_send()
            part_copy(m, j).wait_send()

            @pl.when(jnp.logical_not(last))
            def _():
                z_copy(m, j).wait_send()

            return c

        lax.fori_loop(0, chunks * per_chunk, one, 0)

        def heads(g, c):
            @pl.when(sends_two)
            def _():
                halo_two(m, g).wait_send()

            @pl.when(sends_three)
            def _():
                halo_three(m, g).wait_send()

            @pl.when(passes_one)
            def _():
                pass_one(m, g).wait_send()

            @pl.when(even)
            def _():
                halo_mate(m, g).wait_send()

            @pl.when(passes_pair)
            def _():
                pass_pair(m, g).wait_send()

            return c

        lax.fori_loop(0, kv_heads, heads, 0)
        return carry

    lax.fori_loop(0, micros, drain, 0)


def doc_lookup(ids, token_index):
    blocks = ids.shape[1]
    start = jnp.sum((ids[:, None, :] < ids[:, :, None]).astype(jnp.int32), axis=2)
    block_of = jnp.clip(token_index // BLOCK, 0, blocks - 1)
    onehot = (block_of[:, None] == jnp.arange(blocks, dtype=jnp.int32)[None, :]).astype(jnp.int32)
    start_of = jnp.sum(onehot[None] * start[:, None, :], axis=2)
    doc_of = jnp.sum(onehot[None] * ids[:, None, :], axis=2)
    return token_index[None] - start_of * BLOCK, doc_of


def tables(doc_ids, rows):
    ctx = lax.axis_index("ctx")
    token_index = ctx * 2 * rows + jnp.arange(2 * rows, dtype=jnp.int32)
    position, query_doc = doc_lookup(doc_ids, token_index)
    frequency = ROPE_BASE ** (-(jnp.arange(HEAD // 2, dtype=jnp.float32) * 2.0) / HEAD)
    angles = position.astype(jnp.float32)[:, :, None] * frequency
    cosine, sine = jnp.cos(angles), jnp.sin(angles)
    key_index = (2 * ctx - HALO) * rows + jnp.arange((HALO + 2) * rows, dtype=jnp.int32)
    unused, key_doc = doc_lookup(doc_ids, key_index)
    biases = []
    for t in range(2):
        q_at = token_index[t * rows : (t + 1) * rows][:, None]
        k_at = key_index[t * rows : (t + HALO + 1) * rows][None, :]
        q_doc = query_doc[:, t * rows : (t + 1) * rows, None]
        k_doc = key_doc[:, None, t * rows : (t + HALO + 1) * rows]
        allowed = (k_at >= 0) & (k_at <= q_at) & (q_at - k_at < WINDOW)
        biases.append(jnp.where(allowed[None] & (q_doc == k_doc), 0.0, -1e30))
    return (
        jnp.concatenate([cosine, cosine], axis=-1),
        jnp.concatenate([-sine, sine], axis=-1),
        jnp.stack(biases, axis=1).astype(jnp.float32),
    )


def local(x_in, norm_gain, w_query, w_key, value_projection, w_out, doc_ids):
    micros, rows, width = x_in.shape
    ctxs = lax.axis_size("ctx")
    cosine, sine, bias = tables(doc_ids, rows)
    query_cols, key_cols = w_query.shape[2], w_key.shape[2]
    deep = w_key.shape[1]
    query_heads, kv_heads = query_cols // HEAD, key_cols // HEAD
    pieces = width // PIECE
    vmem = pl.BlockSpec(memory_space=pltpu.VMEM)
    hbm = pl.BlockSpec(memory_space=pl.ANY)
    per_piece = pltpu.SemaphoreType.DMA((micros, pieces))
    per_head = pltpu.SemaphoreType.DMA((micros, 3, kv_heads))
    return pl.pallas_call(
        kernel,
        out_shape=jax.ShapeDtypeStruct((1, micros, rows, width), jnp.bfloat16),
        in_specs=[hbm, vmem] + [hbm] * 4 + [vmem] * 3,
        out_specs=hbm,
        scratch_shapes=[
            pltpu.VMEM((width, query_cols), jnp.bfloat16),
            pltpu.VMEM((2, ctxs, deep, key_cols), jnp.bfloat16),
            pltpu.VMEM((2, ctxs, query_cols // 2, deep), jnp.bfloat16),
            pltpu.VMEM((2, width, key_cols), jnp.bfloat16),
            pltpu.VMEM((query_cols, width), jnp.bfloat16),
            pltpu.VMEM((micros, 2, rows, width), jnp.bfloat16),
            pltpu.VMEM((micros, rows, width), jnp.bfloat16),
            pltpu.VMEM((2 * rows, query_cols + 2 * key_cols), jnp.float32),
            pltpu.VMEM((2 * rows, HEAD), jnp.float32),
            pltpu.VMEM((2, query_heads, rows, HEAD), jnp.bfloat16),
            pltpu.VMEM((micros, kv_heads, HALO + 2, 2, rows, HEAD), jnp.bfloat16),
            pltpu.VMEM((2, kv_heads, rows, query_heads // kv_heads * HEAD), jnp.bfloat16),
            pltpu.VMEM((rows, width), jnp.float32),
            pltpu.VMEM((micros, rows, width), jnp.bfloat16),
            pltpu.VMEM((micros, rows, width), jnp.bfloat16),
        ]
        + [per_piece] * 6
        + [per_head] * 2
        + [
            pltpu.SemaphoreType.DMA((4, 15)),
            pltpu.SemaphoreType.DMA((4, ctxs)),
            pltpu.SemaphoreType.DMA((5,)),
            pltpu.SemaphoreType.DMA((micros,)),
        ],
        compiler_params=pltpu.CompilerParams(
            collective_id=0, has_side_effects=True, vmem_limit_bytes=60 * 1024 * 1024
        ),
    )(x_in, norm_gain, w_query, w_key, value_projection, w_out, cosine, sine, bias)


def solution(mesh):
    in_specs = (
        P(None, ("ctx", "tp"), None),
        P("section", None),
        P("section", None, "tp"),
        P("section", "ctx", "tp"),
        P("section", "ctx", "tp"),
        P("section", "tp", "ctx"),
        P(),
    )
    out_specs = P("section", None, ("ctx", "tp"), None)
    return jax.shard_map(local, mesh=mesh, in_specs=in_specs, out_specs=out_specs, check_vma=False)
```

time: 628 us -> 463 us (0.74)
  waiting for transfers between devices: 162 us -> 0 us
  Pallas kernels: 434 us -> 450 us
  between operations: 13.2 us -> 0.13 us
    all_gather x3 -> x0, waiting for transfers between devices: 160 us -> none  [the longest x1 56.1 us: local(): wv = lax.all_gather(value_projection, 'ctx', axis=1, tiled=True)[0]]
    pallas_call x1, Pallas kernels: 434 us -> 450 us  [local(): pl.pallas_call(kernel, out_shape=jax.ShapeDtypeStruct((1, micros, rows, w...]
    all_gather x1 -> x0, local copies, waits for them, and re-layouts: 7.93 us -> none  [local(): wo = lax.all_gather(w_out, 'ctx', axis=2, tiled=True)[0]]
  transfers between devices with their start and end apart: 3 -> 0, of which waited for: 3 -> 0; matrix products, arithmetic and copies ran while one was open for 2% -> 0% of each run, Pallas kernels for 0% -> 0%
where the time goes in v2:
time: 463 us; the launch traced here: 462 us
  Pallas kernels  450 us (97%)
  other arithmetic  7.32 us (2%)
    pallas_call x1, Pallas kernels, local(): pl.pallas_call(kernel, out_shape=jax.ShapeDtypeStruct((1, micros, rows, w...  450 us

profile of v2, /device:TPU:253, one launch (start us, length us, event | category | flops | bytes accessed | tf_op | source)
XLA Modules:
  0.0 462.2 jit_solution(5464673676062678686)
XLA Ops:
  0.0 0.9 convert_reduce_fusion
  1.0 0.8 multiply_reduce_fusion.1
  1.8 0.2 fusion
  2.0 0.2 fusion.1
  2.2 0.8 multiply_reduce_fusion
  3.1 2.0 copy.9.wo_ref
  5.0 0.2 and_select_fusion.1
  5.2 0.2 and_select_fusion
  5.5 1.3 pad_maximum_fusion.bias_ref
  6.8 1.0 fusion.3
  7.7 0.8 pad_maximum_fusion.2.sin_ref
  8.6 0.9 pad_maximum_fusion.1.cos_ref
  9.4 450.2 %shard_map.73 = bf16[1,2,128,2688]{3,2,1,0:T(8,128)(2,1)} custom-call(bf16[2,128,2688]{2,1,0:T(8,128)(2,1)} %x_ref.1, bf16[1,2688]{1,0:T(2,128)(2,1)} %gain_ref.1, bf16[1,2688,1024]{2,1,0:T(8,128)(2,1)} %wq_ref.1, bf16[1,168,512]{2,1,0:T(8,128)(2,1)} %wk_ref.1, bf16[1,168,512]{2,1,0:T(8,128)(2,1)} %wv_ref.1, bf16[1,1024,168]{2,1,0:T(8,128)(2,1)} %copy.9.wo_ref, ...), custom_call_target="tpu_custom_call" | custom-call | tf_op jit(solution)/shard_map/pallas_call | solution.py:537
  459.7 2.5 copy.11
  (11 shorter events, 0.1 us)
